TPU v7x, 32 devices: a whole 2x2x4 slice. The times are simulated.
32 devices in a mesh: layer: 4 (over y, x), lat: 8 (over z, core).
Axes of the slice: x: 2, y: 2, z: 4, core: 2. Of those that a mesh axis runs over, the one named last changes fastest.
Arguments:
- activations: bfloat16 [8, 512, 2048], P(None, None, 'layer'), may hold values from -6 to 6
- targets: bfloat16 [8, 512, 2048], P(None, None, 'layer'), may hold values from -6 to 6
- encoder: bfloat16 [8, 2048, 8192], P(None, 'layer', 'lat'), may hold values from -0.125 to 0.125
- bias: float32 [8, 8192], P(None, 'lat'), may hold values from -3 to 3
- decoder: bfloat16 [36, 8192, 2048], P(None, 'lat', 'layer'), may hold values from -0.75 to 0.75
- active: int32 [8, 512, 64], replicated, may hold values from 0 to 8191, all different within a row
Outputs:
- grad_encoder: bfloat16 [8, 2048, 8192], P(None, 'layer', 'lat')
- grad_bias: float32 [8, 8192], P(None, 'lat')
- grad_decoder: bfloat16 [36, 8192, 2048], P(None, 'lat', 'layer')
Inputs may be any that keep to these rules, and one draw needn't show every extreme that they name: `active`: each row names 64 different latents.
All inputs are finite; a program needn't handle non-finite values.
Results may differ from a plain program's by a relative error of at most 0.0064.
Values may be sent and summed in bfloat16 or wider, within the bound.
A program may use at most 256 MiB of HBM per device.

v0:
```python
import jax
import jax.numpy as jnp
from jax import lax
from jax.sharding import PartitionSpec as P

LAYERS = 8


def pair_index(source, target):
    return source * LAYERS - source * (source - 1) // 2 + (target - source)


def on_device(activations, targets, encoder, bias, decoder, active):
    tokens = activations.shape[1]
    lat_width = encoder.shape[2]
    first = lax.axis_index("lat") * lat_width
    columns = first + jnp.arange(lat_width, dtype=jnp.int32)
    masks = jnp.stack(
        [
            jnp.any(active[source][:, :, None] == columns[None, None, :], axis=1)
            for source in range(LAYERS)
        ]
    ).astype(jnp.float32)
    partial_value = jnp.einsum(
        "ltd,ldf->ltf", activations, encoder, preferred_element_type=jnp.float32
    )
    preact = lax.psum(partial_value, "layer") + bias[:, None, :]
    latent_act = (preact * masks).astype(jnp.bfloat16)
    rebuilt_list = []
    for target in range(LAYERS):
        summed = jnp.dot(
            latent_act[0], decoder[pair_index(0, target)], preferred_element_type=jnp.float32
        )
        for source in range(1, target + 1):
            summed = summed + jnp.dot(
                latent_act[source],
                decoder[pair_index(source, target)],
                preferred_element_type=jnp.float32,
            )
        rebuilt_list.append(summed)
    rebuilt = jnp.stack(rebuilt_list)
    complete = lax.psum(rebuilt, "lat")
    errors = (complete - targets.astype(jnp.float32)).astype(jnp.bfloat16)
    by_tokens = (((0,), (0,)), ((), ()))
    by_width = (((1,), (1,)), ((), ()))
    grad_pairs = []
    for source in range(LAYERS):
        for target in range(source, LAYERS):
            grad_pairs.append(
                lax.dot_general(
                    latent_act[source],
                    errors[target],
                    by_tokens,
                    preferred_element_type=jnp.float32,
                ).astype(jnp.bfloat16)
            )
    grad_decoder = jnp.stack(grad_pairs)
    grad_list = []
    for source in range(LAYERS):
        summed = lax.dot_general(
            errors[source],
            decoder[pair_index(source, source)],
            by_width,
            preferred_element_type=jnp.float32,
        )
        for target in range(source + 1, LAYERS):
            summed = summed + lax.dot_general(
                errors[target],
                decoder[pair_index(source, target)],
                by_width,
                preferred_element_type=jnp.float32,
            )
        grad_list.append(summed)
    grad_partial = jnp.stack(grad_list)
    block_rows = tokens // lax.axis_size("layer")
    share_rows = lax.psum_scatter(grad_partial, "layer", scatter_dimension=1, tiled=True)
    mask_rows = lax.dynamic_slice_in_dim(masks, lax.axis_index("layer") * block_rows, block_rows, 1)
    grad_pre = lax.all_gather(
        (share_rows * mask_rows).astype(jnp.bfloat16), "layer", axis=1, tiled=True
    )
    grad_encoder = jnp.einsum(
        "ltd,ltf->ldf", activations, grad_pre, preferred_element_type=jnp.float32
    ).astype(jnp.bfloat16)
    grad_bias = jnp.sum(grad_pre.astype(jnp.float32), axis=1)
    return (grad_encoder, grad_bias, grad_decoder)


def solution(mesh):
    placed = (
        P(None, None, "layer"),
        P(None, None, "layer"),
        P(None, "layer", "lat"),
        P(None, "lat"),
        P(None, "lat", "layer"),
        P(),
    )
    return jax.shard_map(
        on_device,
        mesh=mesh,
        in_specs=placed,
        out_specs=(P(None, "layer", "lat"), P(None, "lat"), P(None, "lat", "layer")),
        check_vma=False,
    )
```

profile of v0, /device:TPU:0, one launch (start us, length us, event | category | flops | bytes accessed | tf_op | source)
XLA Modules:
  0.0 1017.3 jit_solution(10485353639587241992)
XLA Ops:
  7.2 15.4 %fusion.266 = f32[8,512,1024]{2,1,0:T(8,128)} fusion(bf16[8,512,512]{2,1,0:T(8,128)(2,1)} %param.6, bf16[8,512,1024]{2,1,0:T(8,128)(2,1)} %param.8), kind=kOutput, calls=%fused_computation.385 | convolution fusion | flops 4294967296 | bytes 29360128 | tf_op jit(solution)/shard_map/ltd,ldf->ltf/dot_general | solution.py:24
  25.0 192.2 %compare_reduce_fusion = (pred[512,1024]{1,0:T(8,128)(4,1)S(1)}, pred[512,1024]{1,0:T(8,128)(4,1)S(1)}, pred[512,1024]{1,0:T(8,128)(4,1)S(1)}, pred[512,1024]{1,...) fusion(s32[512,64]{1,0:T(8,128)S(1)} %copy.26, ...), kind=kLoop, calls=%fused_computation | loop fusion | flops 532676608 | bytes 5246976 | tf_op jit(solution)/shard_map/reduce_or | solution.py:20
  223.9 108.9 %all-reduce.3.cloned.1.call-done = f32[8,512,1024]{2,1,0:T(8,128)} async-done(((f32[8,512,1024]{2,1,0:T(8,128)}), f32[8,512,1024]{2,1,0:T(8,128)}) %all-reduce.3.cloned.1.call-update) | async-done | bytes 16777232 | tf_op jit(solution)/shard_map/psum | solution.py:27
  332.8 9.7 select_convert_fusion
  342.5 5.7 fusion.102
  409.9 13.2 %convolution_add_fusion.24 = f32[512,512]{1,0:T(8,128)} fusion(f32[512,512]{1,0:T(8,128)S(1)} %fusion.172, bf16[36,1024,512]{2,1,0:T(8,128)(2,1)S(1)} %bitcast.587, bf16[8,512,1024]{2,1,0:T(8,128)(2,1)S(1)} %select_convert_fusion), kind=kOutput, calls=%fused_computation.99 | convolution fusion | flops 537133056 | bytes 4194304 | tf_op jit(solution)/shard_map/dot_general | solution.py:35
  443.3 176.7 %all-reduce.5.cloned.1.call-done = f32[8,512,512]{2,1,0:T(8,128)} async-done(((f32[8,512,512]{2,1,0:T(8,128)}), f32[8,512,512]{2,1,0:T(8,128)}) %all-reduce.5.cloned.1.call-update) | async-done | bytes 8388624 | tf_op jit(solution)/shard_map/psum | solution.py:42
  619.9 6.0 subtract_convert_fusion
  636.6 3.3 fusion.187
  639.9 3.3 fusion.191
  643.3 3.3 fusion.119
  649.8 3.3 fusion.154
  653.1 3.3 fusion.167
  656.4 3.3 fusion.177
  659.7 3.3 fusion.184
  672.9 3.3 fusion.113
  679.5 3.3 fusion.148
  682.8 3.7 fusion.161
  692.4 3.3 fusion.107
  699.0 3.3 fusion.104
  702.3 5.1 bitcast_dynamic-update-slice_fusion.7
  707.4 7.2 bitcast_dynamic-update-slice_fusion.6
  714.7 3.7 bitcast_dynamic-update-slice_fusion.5
  719.2 3.7 bitcast_dynamic-update-slice_fusion.4
  723.0 3.5 bitcast_dynamic-update-slice_fusion.3
  726.5 3.3 bitcast_dynamic-update-slice_fusion.2
  736.6 153.8 %reduce-scatter.2.cloned.1.call-done = f32[8,128,1024]{2,1,0:T(8,128)} async-done(((f32[8,512,1024]{2,1,0:T(8,128)}), f32[8,128,1024]{2,1,0:T(8,128)}) %reduce-scatter.2.cloned.1.call-update) | async-done | bytes 4194320 | tf_op jit(solution)/shard_map/reduce_scatter | solution.py:76
  890.4 4.6 multiply_convert_fusion
  964.1 18.5 %all-gather.2.cloned.1.call-done = bf16[8,512,1024]{2,1,0:T(8,128)(2,1)} async-done(((bf16[8,128,1024]{2,1,0:T(8,128)(2,1)}), bf16[8,512,1024]{2,1,0:T(8,128)(2,1)}) %all-gather.2.cloned.1.call-update) | async-done | bytes 8388624 | tf_op jit(solution)/shard_map/all_gather | solution.py:78
  982.6 10.5 %convert_bitcast_fusion = bf16[8,512,1024]{1,2,0:T(8,128)(2,1)} fusion(bf16[8,512,1024]{2,1,0:T(8,128)(2,1)} %all-gather.2.cloned.1.call-done, bf16[8,512,512]{2,1,0:T(8,128)(2,1)} %param.6), kind=kOutput, calls=%fused_computation.10 | convolution fusion | flops 4299161600 | bytes 20971520 | tf_op jit(solution)/shard_map/ltd,ltf->ldf/dot_general | solution.py:81
  993.1 11.4 %copy.28 = bf16[8,512,1024]{2,1,0:T(8,128)(2,1)} copy(bf16[8,512,1024]{1,2,0:T(8,128)(2,1)} %convert_bitcast_fusion) | data formatting | bytes 16777216
  1004.4 5.9 convert_reduce_fusion
  (166 shorter events, 203.6 us)
Async XLA Ops:
  7.2 325.6 %all-reduce.3.cloned.1.call-start = ((), (), s32[]{:S(2)}) async-start(), calls=%async_computation.1 | async-start | bytes 33554432 | tf_op jit(solution)/shard_map/psum | solution.py:27
  22.6 1.2 copy-start.10
  22.6 597.4 %all-reduce.5.cloned.1.call-start = ((), (), s32[]{:S(2)}) async-start(), calls=%async_computation.2 | async-start | bytes 16777216 | tf_op jit(solution)/shard_map/psum | solution.py:42
  24.3 308.5 %copy-start.11 = (f32[8,1024]{1,0:T(8,128)S(1)}, f32[8,1024]{1,0:T(8,128)}, u32[]{:S(2)}) copy-start(f32[8,1024]{1,0:T(8,128)} %param.9) | copy-start | bytes 98308
  332.8 38.9 %slice-start = ((s8[37748736]{0:T(1024)(128)(4,1)}), s8[4194304]{0:T(1024)(128)(4,1)S(1)}, s32[]{:S(2)}) async-start(s8[37748736]{0:T(1024)(128)(4,1)} %bitcast.586), calls=%async_computation.5 | async-start | bytes 8388608
  332.8 38.9 %slice-start.1 = ((s8[37748736]{0:T(1024)(128)(4,1)}), s8[4194304]{0:T(1024)(128)(4,1)S(1)}, s32[]{:S(2)}) async-start(s8[37748736]{0:T(1024)(128)(4,1)} %bitcast.586), calls=%async_computation.6 | async-start | bytes 8388608
  332.8 38.9 %slice-start.2 = ((s8[37748736]{0:T(1024)(128)(4,1)}), s8[4194304]{0:T(1024)(128)(4,1)S(1)}, s32[]{:S(2)}) async-start(s8[37748736]{0:T(1024)(128)(4,1)} %bitcast.586), calls=%async_computation.7 | async-start | bytes 8388608
  332.8 38.9 %slice-start.3 = ((s8[37748736]{0:T(1024)(128)(4,1)}), s8[4194304]{0:T(1024)(128)(4,1)S(1)}, s32[]{:S(2)}) async-start(s8[37748736]{0:T(1024)(128)(4,1)} %bitcast.586), calls=%async_computation.8 | async-start | bytes 8388608
  342.5 99.0 %copy-start.9 = (bf16[8,512,1024]{2,1,0:T(8,128)(2,1)}, bf16[8,512,1024]{2,1,0:T(8,128)(2,1)S(1)}, u32[]{:S(2)}) copy-start(bf16[8,512,1024]{2,1,0:T(8,128)(2,1)S(1)} %select_convert_fusion) | copy-start | bytes 25165828
  342.5 29.2 %slice-start.4 = ((s8[37748736]{0:T(1024)(128)(4,1)}), s8[4194304]{0:T(1024)(128)(4,1)S(1)}, s32[]{:S(2)}) async-start(s8[37748736]{0:T(1024)(128)(4,1)} %bitcast.586), calls=%async_computation.9 | async-start | bytes 8388608
  350.3 21.4 %slice-start.5 = ((s8[37748736]{0:T(1024)(128)(4,1)}), s8[4194304]{0:T(1024)(128)(4,1)S(1)}, s32[]{:S(2)}) async-start(s8[37748736]{0:T(1024)(128)(4,1)} %bitcast.586), calls=%async_computation.10 | async-start | bytes 8388608
  356.4 15.4 %slice-start.6 = ((s8[37748736]{0:T(1024)(128)(4,1)}), s8[4194304]{0:T(1024)(128)(4,1)S(1)}, s32[]{:S(2)}) async-start(s8[37748736]{0:T(1024)(128)(4,1)} %bitcast.586), calls=%async_computation.11 | async-start | bytes 8388608
  360.4 11.4 %slice-start.7 = ((s8[37748736]{0:T(1024)(128)(4,1)}), s8[4194304]{0:T(1024)(128)(4,1)S(1)}, s32[]{:S(2)}) async-start(s8[37748736]{0:T(1024)(128)(4,1)} %bitcast.586), calls=%async_computation.12 | async-start | bytes 8388608
  366.4 5.4 slice-start.8
  426.0 10.5 %copy-start.13 = (f32[512,512]{1,0:T(8,128)S(1)}, f32[512,512]{1,0:T(8,128)}, u32[]{:S(2)}) copy-start(f32[512,512]{1,0:T(8,128)} %convolution_add_fusion.19) | copy-start | bytes 3145732
  427.7 10.5 %copy-start.12 = (f32[512,512]{1,0:T(8,128)S(1)}, f32[512,512]{1,0:T(8,128)}, u32[]{:S(2)}) copy-start(f32[512,512]{1,0:T(8,128)} %convolution_add_fusion.14) | copy-start | bytes 3145732
  443.2 447.2 %reduce-scatter.2.cloned.1.call-start = ((), (), s32[]{:S(2)}) async-start(), calls=%async_computation.3 | async-start | bytes 20971520 | tf_op jit(solution)/shard_map/reduce_scatter | solution.py:76
  626.0 107.1 %copy-start = (bf16[8,512,512]{2,1,0:T(8,128)(2,1)}, bf16[8,512,512]{2,1,0:T(8,128)(2,1)S(1)}, u32[]{:S(2)}) copy-start(bf16[8,512,512]{2,1,0:T(8,128)(2,1)S(1)} %subtract_convert_fusion) | copy-start | bytes 12582916
  714.7 3.7 copy-start.5
  714.7 3.7 copy-start.6
  714.7 3.7 copy-start.7
  714.7 4.5 copy-start.8
  719.2 7.2 copy-start.3
  719.2 7.2 copy-start.4
  723.0 6.8 copy-start.2
  736.4 246.2 %all-gather.2.cloned.1.call-start = ((), (), s32[]{:S(2)}) async-start(), calls=%async_computation.4 | async-start | bytes 10485760 | tf_op jit(solution)/shard_map/all_gather | solution.py:78
  895.0 6.5 copy-start.1
  898.2 12.4 %slice-start.9 = ((s8[8388608]{0:T(1024)(128)(4,1)}), s8[4194304]{0:T(1024)(128)(4,1)S(1)}, s32[]{:S(2)}) async-start(s8[8388608]{0:T(1024)(128)(4,1)} %bitcast.588), calls=%async_computation.14 | async-start | bytes 8388608
  904.5 6.1 slice-start.10
Sparse Core Ops, SparseCore 0:
  22.7 310.0 all-reduce.2
  443.3 176.5 all-reduce.4
  736.5 153.8 reduce-scatter.1
  895.1 87.4 all-gather.1
where the time goes:
time: 1030 us; the launch traced here: 1020 us
  waiting for transfers between devices  458 us (44%)
  matrix products  305 us (30%)
  other arithmetic  218 us (21%)
  local copies, waits for them, and re-layouts  21.2 us (2%)
  between operations  14.7 us (1%)
    reduce_or x1, other arithmetic, on_device(): jnp.any(active[source][:, :, None] == columns[None, None, :], axis=1)  192 us
    psum x1, waiting for transfers between devices, on_device(): complete = lax.psum(rebuilt, 'lat')  177 us
    reduce_scatter x1, waiting for transfers between devices, on_device(): lax.psum_scatter(grad_partial, 'layer', scatter_dimension=1, tiled=True)  154 us
    psum x1, waiting for transfers between devices, on_device(): preact = lax.psum(partial_value, 'layer') + bias[:, None, :]  109 us
    dot_general x28, matrix products, on_device(): lax.dot_general(errors[target], decoder[pair_index(source, target)], by_w...  85.2 us
    dot_general x28, matrix products, on_device(): jnp.dot(latent_act[source], decoder[pair_index(source, target)], preferre...  76.7 us
    dot_general x36, matrix products, on_device(): lax.dot_general(latent_act[source], errors[target], by_tokens, preferred_...  69.1 us
    dot_general x8, matrix products, on_device(): lax.dot_general(errors[source], decoder[pair_index(source, source)], by_w...  24.2 us
  transfers between devices with their start and end apart: 4, of which 4 were waited for; matrix products, arithmetic and copies ran while one was open for 26% of the time, Pallas kernels for 0%

commit v1 on v0

--- a/solution.py
+++ b/solution.py
@@ -24,7 +24,7 @@
     partial_value = jnp.einsum(
         "ltd,ldf->ltf", activations, encoder, preferred_element_type=jnp.float32
     )
-    preact = lax.psum(partial_value, "layer") + bias[:, None, :]
+    preact = jnp.sum(lax.all_gather(partial_value, "layer"), axis=0) + bias[:, None, :]
     latent_act = (preact * masks).astype(jnp.bfloat16)
     rebuilt_list = []
     for target in range(LAYERS):

time: 1030 us -> 1310 us (1.27)
  waiting for transfers between devices: 458 us -> 726 us
  other arithmetic: 218 us -> 247 us
    all_gather x0 -> x1, waiting for transfers between devices: none -> 378 us  [on_device(): lax.all_gather(partial_value, 'layer')]
    psum x1 -> x0, waiting for transfers between devices: 109 us -> none  [on_device(): preact = lax.psum(partial_value, 'layer') + bias[:, None, :]]
    reduce_sum x0 -> x1, other arithmetic: none -> 28.1 us  [on_device(): jnp.sum(lax.all_gather(partial_value, 'layer'), axis=0) + bias[:, None, :]]
  transfers between devices with their start and end apart: 4 -> 4, of which waited for: 4 -> 4; matrix products, arithmetic and copies ran while one was open for 26% -> 21% of each run, Pallas kernels for 0% -> 0%
where the time goes in v1:
time: 1310 us; the launch traced here: 1300 us
  waiting for transfers between devices  726 us (55%)
  matrix products  293 us (22%)
  other arithmetic  247 us (19%)
  local copies, waits for them, and re-layouts  21.1 us (2%)
  between operations  14.5 us (1%)
    all_gather x1, waiting for transfers between devices, on_device(): lax.all_gather(partial_value, 'layer')  378 us
    reduce_or x1, other arithmetic, on_device(): jnp.any(active[source][:, :, None] == columns[None, None, :], axis=1)  193 us
    psum x1, waiting for transfers between devices, on_device(): complete = lax.psum(rebuilt, 'lat')  176 us
    reduce_scatter x1, waiting for transfers between devices, on_device(): lax.psum_scatter(grad_partial, 'layer', scatter_dimension=1, tiled=True)  154 us
    dot_general x28, matrix products, on_device(): lax.dot_general(errors[target], decoder[pair_index(source, target)], by_w...  85.2 us
    dot_general x36, matrix products, on_device(): lax.dot_general(latent_act[source], errors[target], by_tokens, preferred_...  69.1 us
    dot_general x28, matrix products, on_device(): jnp.dot(latent_act[source], decoder[pair_index(source, target)], preferre...  65.4 us
    reduce_sum x1, other arithmetic, on_device(): jnp.sum(lax.all_gather(partial_value, 'layer'), axis=0) + bias[:, None, :]  28.1 us
  transfers between devices with their start and end apart: 4, of which 4 were waited for; matrix products, arithmetic and copies ran while one was open for 21% of the time, Pallas kernels for 0%

profile of v1, /device:TPU:0, one launch (start us, length us, event | category | flops | bytes accessed | tf_op | source)
XLA Modules:
  0.0 1302.3 jit_solution(3333666228966591116)
XLA Ops:
  7.2 15.4 %fusion.266 = f32[8,512,1024]{2,1,0:T(8,128)} fusion(bf16[8,512,512]{2,1,0:T(8,128)(2,1)} %param.6, bf16[8,512,1024]{2,1,0:T(8,128)(2,1)} %param.8), kind=kOutput, calls=%fused_computation.385 | convolution fusion | flops 4294967296 | bytes 29360128 | tf_op jit(solution)/shard_map/ltd,ldf->ltf/dot_general | solution.py:24
  24.9 192.8 %compare_reduce_fusion = (pred[512,1024]{1,0:T(8,128)(4,1)S(1)}, pred[512,1024]{1,0:T(8,128)(4,1)S(1)}, pred[512,1024]{1,0:T(8,128)(4,1)S(1)}, pred[512,1024]{1,...) fusion(s32[512,64]{1,0:T(8,128)S(1)} %copy.36, ...), kind=kLoop, calls=%fused_computation | loop fusion | flops 532676608 | bytes 5246976 | tf_op jit(solution)/shard_map/reduce_or | solution.py:20
  224.5 377.7 %all-gather.6.cloned.1.call-done = f32[32,512,1024]{2,1,0:T(8,128)} async-done(((f32[8,512,1024]{2,1,0:T(8,128)}), f32[32,512,1024]{2,1,0:T(8,128)}) %all-gather.6.cloned.1.call-update) | async-done | bytes 67108880 | tf_op jit(solution)/shard_map/all_gather | solution.py:27
  602.1 28.1 %reduce_sum.18 = f32[8,512,1024]{2,1,0:T(8,128)} reduce(f32[4,8,512,1024]{3,2,1,0:T(8,128)} %bitcast.16, f32[]{:T(128)} %constant.6.clone.1), dimensions={0}, to_apply=%region_8.0 | reduce | flops 12582912 | bytes 83886080 | tf_op jit(solution)/shard_map/reduce_sum | solution.py:27
  630.3 9.8 select_convert_fusion
  640.1 5.7 fusion.102
  729.5 175.7 %all-reduce.2.cloned.1.call-done = f32[8,512,512]{2,1,0:T(8,128)} async-done(((f32[8,512,512]{2,1,0:T(8,128)}), f32[8,512,512]{2,1,0:T(8,128)}) %all-reduce.2.cloned.1.call-update) | async-done | bytes 8388624 | tf_op jit(solution)/shard_map/psum | solution.py:42
  905.1 6.0 subtract_convert_fusion
  921.8 3.3 fusion.187
  925.1 3.3 fusion.191
  928.4 3.3 fusion.119
  935.0 3.3 fusion.154
  941.6 3.3 fusion.177
  944.9 3.3 fusion.184
  958.0 3.3 fusion.113
  961.4 3.3 fusion.132
  967.9 3.7 fusion.161
  977.5 3.4 fusion.107
  980.9 3.3 fusion.126
  987.5 5.1 bitcast_dynamic-update-slice_fusion.7
  992.5 7.3 bitcast_dynamic-update-slice_fusion.6
  999.8 3.7 bitcast_dynamic-update-slice_fusion.5
  1004.3 3.7 bitcast_dynamic-update-slice_fusion.4
  1008.1 3.5 bitcast_dynamic-update-slice_fusion.3
  1011.6 3.3 bitcast_dynamic-update-slice_fusion.2
  1018.2 3.3 bitcast_dynamic-update-slice_fusion
  1021.7 153.8 %reduce-scatter.2.cloned.1.call-done = f32[8,128,1024]{2,1,0:T(8,128)} async-done(((f32[8,512,1024]{2,1,0:T(8,128)}), f32[8,128,1024]{2,1,0:T(8,128)}) %reduce-scatter.2.cloned.1.call-update) | async-done | bytes 4194320 | tf_op jit(solution)/shard_map/reduce_scatter | solution.py:76
  1175.5 4.6 multiply_convert_fusion
  1249.2 18.5 %all-gather.4.cloned.1.call-done = bf16[8,512,1024]{2,1,0:T(8,128)(2,1)} async-done(((bf16[8,128,1024]{2,1,0:T(8,128)(2,1)}), bf16[8,512,1024]{2,1,0:T(8,128)(2,1)}) %all-gather.4.cloned.1.call-update) | async-done | bytes 8388624 | tf_op jit(solution)/shard_map/all_gather | solution.py:78
  1267.7 10.5 convert_bitcast_fusion
  1278.2 11.4 copy.38
  1289.5 5.9 convert_reduce_fusion
  (167 shorter events, 205.4 us)
Async XLA Ops:
  7.2 595.0 %all-gather.6.cloned.1.call-start = ((), (), s32[]{:S(2)}) async-start(), calls=%async_computation.4 | async-start | bytes 83886080 | tf_op jit(solution)/shard_map/all_gather | solution.py:27
  22.6 1.2 copy-start.10
  22.6 882.5 %all-reduce.2.cloned.1.call-start = ((), (), s32[]{:S(2)}) async-start(), calls=%async_computation.1 | async-start | bytes 16777216 | tf_op jit(solution)/shard_map/psum | solution.py:42
  602.1 28.1 %copy-start.11 = (f32[8,1024]{1,0:T(8,128)S(1)}, f32[8,1024]{1,0:T(8,128)}, u32[]{:S(2)}) copy-start(f32[8,1024]{1,0:T(8,128)} %param.9) | copy-start | bytes 98308
  630.3 38.9 %slice-start = ((s8[37748736]{0:T(1024)(128)(4,1)}), s8[4194304]{0:T(1024)(128)(4,1)S(1)}, s32[]{:S(2)}) async-start(s8[37748736]{0:T(1024)(128)(4,1)} %bitcast.587), calls=%async_computation.5 | async-start | bytes 8388608
  630.3 38.9 %slice-start.1 = ((s8[37748736]{0:T(1024)(128)(4,1)}), s8[4194304]{0:T(1024)(128)(4,1)S(1)}, s32[]{:S(2)}) async-start(s8[37748736]{0:T(1024)(128)(4,1)} %bitcast.587), calls=%async_computation.6 | async-start | bytes 8388608
  630.3 39.0 %slice-start.2 = ((s8[37748736]{0:T(1024)(128)(4,1)}), s8[4194304]{0:T(1024)(128)(4,1)S(1)}, s32[]{:S(2)}) async-start(s8[37748736]{0:T(1024)(128)(4,1)} %bitcast.587), calls=%async_computation.7 | async-start | bytes 8388608
  630.3 39.0 %slice-start.3 = ((s8[37748736]{0:T(1024)(128)(4,1)}), s8[4194304]{0:T(1024)(128)(4,1)S(1)}, s32[]{:S(2)}) async-start(s8[37748736]{0:T(1024)(128)(4,1)} %bitcast.587), calls=%async_computation.8 | async-start | bytes 8388608
  640.1 87.6 %copy-start.9 = (bf16[8,512,1024]{2,1,0:T(8,128)(2,1)}, bf16[8,512,1024]{2,1,0:T(8,128)(2,1)S(1)}, u32[]{:S(2)}) copy-start(bf16[8,512,1024]{2,1,0:T(8,128)(2,1)S(1)} %select_convert_fusion) | copy-start | bytes 25165828
  640.1 29.1 %slice-start.4 = ((s8[37748736]{0:T(1024)(128)(4,1)}), s8[4194304]{0:T(1024)(128)(4,1)S(1)}, s32[]{:S(2)}) async-start(s8[37748736]{0:T(1024)(128)(4,1)} %bitcast.587), calls=%async_computation.9 | async-start | bytes 8388608
  647.8 21.4 %slice-start.5 = ((s8[37748736]{0:T(1024)(128)(4,1)}), s8[4194304]{0:T(1024)(128)(4,1)S(1)}, s32[]{:S(2)}) async-start(s8[37748736]{0:T(1024)(128)(4,1)} %bitcast.587), calls=%async_computation.10 | async-start | bytes 8388608
  653.9 15.4 %slice-start.6 = ((s8[37748736]{0:T(1024)(128)(4,1)}), s8[4194304]{0:T(1024)(128)(4,1)S(1)}, s32[]{:S(2)}) async-start(s8[37748736]{0:T(1024)(128)(4,1)} %bitcast.587), calls=%async_computation.11 | async-start | bytes 8388608
  657.9 11.4 slice-start.7
  663.9 5.4 slice-start.8
  712.2 10.5 copy-start.13
  713.9 10.5 copy-start.12
  729.4 446.1 %reduce-scatter.2.cloned.1.call-start = ((), (), s32[]{:S(2)}) async-start(), calls=%async_computation.2 | async-start | bytes 20971520 | tf_op jit(solution)/shard_map/reduce_scatter | solution.py:76
  911.2 107.0 %copy-start = (bf16[8,512,512]{2,1,0:T(8,128)(2,1)}, bf16[8,512,512]{2,1,0:T(8,128)(2,1)S(1)}, u32[]{:S(2)}) copy-start(bf16[8,512,512]{2,1,0:T(8,128)(2,1)S(1)} %subtract_convert_fusion) | copy-start | bytes 12582916
  999.8 3.7 copy-start.5
  999.8 3.7 copy-start.6
  999.8 3.7 copy-start.7
  999.8 4.5 copy-start.8
  1004.3 7.2 copy-start.3
  1004.3 7.2 copy-start.4
  1008.1 6.8 copy-start.2
  1021.5 246.2 %all-gather.4.cloned.1.call-start = ((), (), s32[]{:S(2)}) async-start(), calls=%async_computation.3 | async-start | bytes 10485760 | tf_op jit(solution)/shard_map/all_gather | solution.py:78
  1180.1 6.5 copy-start.1
  1183.3 12.4 slice-start.9
  1189.7 6.1 slice-start.10
Sparse Core Ops, SparseCore 0:
  22.7 579.3 all-gather.5
  729.5 175.5 all-reduce.1
  1021.6 153.8 reduce-scatter.1
  1180.2 87.4 all-gather.3
